TPU v7x, 32 devices: a whole 2x2x4 slice. The times are simulated.
32 devices in a mesh: energy: 8 (over y, x, core), kpt: 4 (over z).
Axes of the slice: x: 2, y: 2, z: 4, core: 2. Of those that a mesh axis runs over, the one named last changes fastest.
Arguments:
- density: bfloat16 [32, 4, 64, 3072], P('energy', 'kpt'), may hold values from -6 to 6
- quad_weights: float32 [32, 4], P('energy', 'kpt'), may hold values from 0.044194173 to 0.17677669
- orbital_cells: int32 [64, 3072], replicated, may hold values from 0 to 131071
- fixed_charge: float32 [512, 64, 256], P('energy', 'kpt'), may hold values from -16 to 16
- gate_mask: int32 [512, 64, 256], P('energy', 'kpt'), may hold values 0 or 1
- gate_voltage: float32 [512], P('energy'), may hold values from -1 to 1
Outputs:
- potential: float32 [512, 64, 256], P('energy', 'kpt')
- band_shift: float32 [32, 4, 64], P('energy', 'kpt')
Inputs may be any that keep to these rules, and one draw needn't show every extreme that they name: `orbital_cells`: each entry is s * 64 * 256 + y * 256 + z, a cell of one of the layer's 8 planes.
All inputs are finite; a program needn't handle non-finite values. No bound on the sum of `gate_mask` on one device may be relied on, other than what follows from the above.
Results may differ from a plain program's by a relative error of at most 0.0003.
Values sent between devices are 32-bit elements; how exact they have to be, the bound alone decides.
A program may use at most 64 MiB of HBM per device.

v0:
```python
import jax
import jax.numpy as jnp
from jax import lax
from jax.sharding import PartitionSpec as P

LAYER_DEV = 8
SUB = 8
ITERS = 2


PENALTY = 4.0


def with_halo(block, sides, width):
    for axis, dim in sides:
        count = lax.axis_size(axis)
        forward = [(i, i + 1) for i in range(count - 1)]
        backward = [(target, source) for source, target in forward]
        low = lax.ppermute(
            lax.slice_in_dim(block, block.shape[dim] - width, None, axis=dim), axis, forward
        )
        high = lax.ppermute(lax.slice_in_dim(block, 0, width, axis=dim), axis, backward)
        block = jnp.concatenate([low, block, high], axis=dim)
    return block


def operate(values_field, diagonal):
    padded = with_halo(values_field, (("energy", 0), ("kpt", 1)), 1)
    padded = jnp.pad(padded, ((0, 0), (0, 0), (1, 1)))
    beside = padded[2:, 1:-1, 1:-1] + padded[:-2, 1:-1, 1:-1]
    beside = beside + padded[1:-1, 2:, 1:-1] + padded[1:-1, :-2, 1:-1]
    beside = beside + padded[1:-1, 1:-1, 2:] + padded[1:-1, 1:-1, :-2]
    return diagonal * values_field - beside


def paired_sums(residual, image):
    return lax.psum((jnp.sum(residual * residual), jnp.sum(residual * image)), ("energy", "kpt"))


def window_index(map_rows, kpt_index, planes, cross_y, width_y, depth_z):
    section = cross_y * depth_z
    within = map_rows % section
    column = within // depth_z - kpt_index * width_y
    inside = (column >= 0) & (column < width_y)
    layer_rows = lax.broadcasted_iota(jnp.int32, map_rows.shape, 0)
    flat_cell = (
        (layer_rows * planes + map_rows // section) * width_y + jnp.clip(column, 0, width_y - 1)
    ) * depth_z + within % depth_z
    return (flat_cell, inside)


def per_device(density, quad_weights, orbital_cells, fixed_charge, gate_mask, gate_voltage):
    planes_dev, width_y, depth_z = fixed_charge.shape
    kpt_index = lax.axis_index("kpt")
    cross_y = width_y * lax.axis_size("kpt")
    occupancy = jnp.einsum(
        "ek,eklo->lo", quad_weights, density.astype(jnp.float32), precision=lax.Precision.HIGHEST
    )
    partial_rows = lax.psum_scatter(occupancy, "energy", scatter_dimension=0, tiled=True)
    slab_occupancy = lax.psum(partial_rows, "kpt")
    slab_cells = lax.dynamic_slice_in_dim(
        orbital_cells, lax.axis_index("energy") * LAYER_DEV, LAYER_DEV, 0
    )
    flat_cell, inside = window_index(slab_cells, kpt_index, SUB, cross_y, width_y, depth_z)
    deposit = jax.ops.segment_sum(
        jnp.where(inside, slab_occupancy, 0.0).reshape(-1),
        flat_cell.reshape(-1),
        num_segments=planes_dev * width_y * depth_z,
    )
    charge = deposit.reshape(planes_dev, width_y, depth_z)
    gated = gate_mask.astype(jnp.float32)
    diagonal = 6.0 + PENALTY * gated
    right_side = fixed_charge - charge + PENALTY * gated * gate_voltage[:, None, None]
    potential = jnp.zeros_like(right_side)
    residual = right_side
    image = operate(residual, diagonal)
    norm_now, product = paired_sums(residual, image)
    alpha = norm_now / product
    direction = residual
    along = image
    for sweep_index in range(ITERS):
        potential = potential + alpha * direction
        residual = residual - alpha * along
        if sweep_index + 1 < ITERS:
            image = operate(residual, diagonal)
            norm_next, product = paired_sums(residual, image)
            ratio = norm_next / norm_now
            alpha = norm_next / (product - ratio * norm_next / alpha)
            direction = residual + ratio * direction
            along = image + ratio * along
            norm_now = norm_next
    local_values = jnp.where(inside, jnp.take(potential.reshape(-1), flat_cell), 0.0)
    orbital_potential = lax.psum(local_values, "kpt")
    factor = density.shape[3] ** (-0.5)
    block = density.astype(jnp.float32)
    band_shift = (
        jnp.einsum(
            "eklo,lo->ekl",
            block,
            lax.all_gather(orbital_potential, "energy", axis=0, tiled=True),
            precision=lax.Precision.HIGHEST,
        )
        * factor
    )
    return (potential, band_shift)


def solution(mesh):
    in_specs = (
        P("energy", "kpt", None, None),
        P("energy", "kpt"),
        P(),
        P("energy", "kpt", None),
        P("energy", "kpt", None),
        P("energy"),
    )
    out_specs = (P("energy", "kpt", None), P("energy", "kpt", None))
    return jax.shard_map(
        per_device, mesh=mesh, in_specs=in_specs, out_specs=out_specs, check_vma=False
    )
```

profile of v0, /device:TPU:1, one launch (start us, length us, event | category | flops | bytes accessed | tf_op | source)
XLA Modules:
  0.0 549.3 jit_solution(11437265235670384205)
XLA Ops:
  7.2 0.0 copy-start
  7.2 0.0 reduce-scatter.2.cloned.1.call-start
  7.2 1.4 copy-done
  8.6 3.8 fusion.3
  12.4 1.0 copy.38
  13.4 0.0 reduce-scatter.2.cloned.1.call-update
  13.4 0.0 all-reduce.7.cloned.1.call-start
  13.5 1.1 fusion.26
  14.6 35.4 %reduce-scatter.2.cloned.1.call-done = f32[8,3072]{1,0:T(8,128)} async-done(((f32[64,3072]{1,0:T(8,128)}), f32[8,3072]{1,0:T(8,128)}) %reduce-scatter.2.cloned.1.call-update) | async-done | bytes 98320 | tf_op jit(solution)/shard_map/reduce_scatter | solution.py:59
  50.0 0.0 all-reduce.7.cloned.1.call-update
  50.1 0.0 all-reduce.9.cloned.1.call-start
  50.1 0.0 copy-done.5
  50.2 35.1 %all-reduce.7.cloned.1.call-done = f32[8,3072]{1,0:T(8,128)} async-done(((f32[8,3072]{1,0:T(8,128)}), f32[8,3072]{1,0:T(8,128)}) %all-reduce.7.cloned.1.call-update) | async-done | bytes 98320 | tf_op jit(solution)/shard_map/psum | solution.py:60
  85.3 1.1 select_bitcast_fusion
  86.4 128.7 %scatter_custom_fusion = f32[262144]{0:T(1024)S(1)} fusion(s32[24576]{0:T(1024)S(1)} %bitcast.33, f32[24576]{0:T(1024)S(1)} %bitcast.34, f32[]{:T(128)} %constant.72.clone.1), kind=kCustom, calls=%fused_computation.56 | custom fusion | flops 24576 | bytes 1048580 | tf_op jit(solution)/shard_map/scatter-add | solution.py:65
  215.1 1.3 reshape.32
  216.3 2.1 multiply_add_fusion.2
  218.5 5.7 %collective-permute-start.1 = (f32[1,16,256]{2,1,0:T(8,128)S(1)}, f32[1,16,256]{2,1,0:T(8,128)S(1)}, u32[]{:S(2)}, u32[]{:S(2)}) collective-permute-start(f32[1,16,256]{2,1,0:T(8,128)S(1)} %get-tuple-element.24), channel_id=1, source_target_pairs={{0,4},{4,8},{8,12},{12,16},{16,20},{20,24},{24,28},{1,5},{5,9},{9,... | collective-permute-start | bytes 49160 | tf_op jit(solution)/shard_map/ppermute | solution.py:19
  224.2 0.0 copy-start.2
  224.2 2.1 collective-permute-start
  226.3 0.0 collective-permute-done.1
  226.3 3.1 collective-permute-done
  229.4 0.1 pad_maximum_fusion.19
  229.5 1.3 collective-permute-start.2
  230.8 4.0 collective-permute-start.3
  234.8 0.0 collective-permute-done.2
  234.8 0.1 copy.12
  234.9 1.3 collective-permute-done.3
  236.2 0.1 copy.14
  236.3 1.2 select_maximum_fusion.4
  237.5 0.0 copy-done.2
  237.6 2.6 multiply_reduce_fusion.1
  240.2 40.1 %all-reduce.3 = (f32[]{:T(128)}, f32[]{:T(128)}) all-reduce(f32[]{:T(128)} %get-tuple-element.7, f32[]{:T(128)} %get-tuple-element.6), channel_id=1, replica_groups=mesh['energy'=8,'kpt'=4] {'energy','kpt'}, use_global_device_ids=true, to_apply=%region_4.5 | all-reduce | flops 2 | bytes 16 | tf_op jit(solution)/shard_map/psum | solution.py:37
  281.6 1.5 multiply_subtract_fusion
  283.0 0.0 copy-start.1
  283.0 5.1 collective-permute-start.5
  288.1 1.9 collective-permute-start.4
  290.1 0.0 collective-permute-done.5
  290.1 3.1 collective-permute-done.4
  293.2 0.1 pad_maximum_fusion.16
  293.3 0.0 copy-start.3
  293.3 1.4 collective-permute-start.6
  294.7 4.0 collective-permute-start.7
  298.8 0.0 collective-permute-done.6
  298.8 0.1 copy.18
  298.9 1.3 collective-permute-done.7
  300.1 0.1 copy.20
  300.2 1.3 select_maximum_fusion
  301.5 0.0 copy-done.1
  301.5 0.0 copy-done.3
  301.5 1.7 fusion.7
  303.1 40.6 %all-reduce.2 = (f32[]{:T(128)}, f32[]{:T(128)}) all-reduce(f32[]{:T(128)} %get-tuple-element.5, f32[]{:T(128)} %get-tuple-element.4), channel_id=1, replica_groups=mesh['energy'=8,'kpt'=4] {'energy','kpt'}, use_global_device_ids=true, to_apply=%region_8.9 | all-reduce | flops 2 | bytes 16 | tf_op jit(solution)/shard_map/psum | solution.py:37
  348.1 1.5 multiply_add_fusion
  349.6 0.0 copy-start.4
  349.6 1.0 copy-done.4
  350.6 0.5 copy.29
  351.1 135.5 %gather_fusion = f32[24576]{0:T(1024)S(1)} fusion(f32[262144]{0:T(1024)S(1)} %bitcast.27, s32[24576]{0:T(1024)S(1)} %broadcast_clamp_fusion), kind=kCustom, calls=%fused_computation | custom fusion | bytes 294912 | tf_op jit(solution)/shard_map/jit(_take)/gather | solution.py:92
  486.7 0.7 select_select_fusion
  487.3 0.0 all-reduce.9.cloned.1.call-update
  487.4 34.1 %all-reduce.9.cloned.1.call-done = f32[8,3072]{1,0:T(8,128)} async-done(((f32[8,3072]{1,0:T(8,128)}), f32[8,3072]{1,0:T(8,128)}) %all-reduce.9.cloned.1.call-update) | async-done | bytes 98320 | tf_op jit(solution)/shard_map/psum | solution.py:93
  521.5 13.3 %all_gather.3 = f32[64,3072]{1,0:T(8,128)S(1)} all-gather(f32[8,3072]{1,0:T(8,128)} %all-reduce.9.cloned.1.call-done), channel_id=1, replica_groups=mesh['energy'=8,'kpt'=4] {'energy'}, dimensions={0}, use_global_device_ids=true | all-gather | bytes 884736 | tf_op jit(solution)/shard_map/all_gather | solution.py:100
  534.7 7.4 %fusion.1 = f32[64,1,4]{2,1,0:T(1,128)S(1)} fusion(bf16[4,64,3072]{2,1,0:T(8,128)(2,1)S(1)} %bitcast.26, f32[64,3072,1]{1,0,2:T(8,128)S(1)} %bitcast.31), kind=kOutput, calls=%fused_computation.13 | convolution fusion | flops 9437184 | bytes 2360320 | tf_op jit(solution)/shard_map/eklo,lo->ekl/dot_general | solution.py:97
  542.1 0.1 copy.26
  542.1 0.6 bitcast_multiply_fusion
  (14 shorter events, 0.2 us)
Async XLA Ops:
  7.2 1.4 copy-start
  7.2 42.9 %reduce-scatter.2.cloned.1.call-start = ((), (), s32[]{:S(2)}) async-start(), calls=%async_computation.1 | async-start | bytes 884736 | tf_op jit(solution)/shard_map/reduce_scatter | solution.py:59
  8.6 41.5 %copy-start.5 = (f32[64]{0:T(128)S(1)}, f32[64]{0:T(128)}, u32[]{:S(2)}) copy-start(f32[64]{0:T(128)} %param.11) | copy-start | bytes 772
  13.4 71.9 %all-reduce.7.cloned.1.call-start = ((), (), s32[]{:S(2)}) async-start(), calls=%async_computation.2 | async-start | bytes 196608 | tf_op jit(solution)/shard_map/psum | solution.py:60
  50.1 471.4 %all-reduce.9.cloned.1.call-start = ((), (), s32[]{:S(2)}) async-start(), calls=%async_computation.3 | async-start | bytes 196608 | tf_op jit(solution)/shard_map/psum | solution.py:93
  218.5 7.8 %collective-permute-start.1 = (f32[1,16,256]{2,1,0:T(8,128)S(1)}, f32[1,16,256]{2,1,0:T(8,128)S(1)}, u32[]{:S(2)}, u32[]{:S(2)}) collective-permute-start(f32[1,16,256]{2,1,0:T(8,128)S(1)} %get-tuple-element.24), channel_id=1, source_target_pairs={{0,4},{4,8},{8,12},{12,16},{16,20},{20,24},{24,28},{1,5},{5,9},{9,... | collective-permute-start | bytes 49160 | tf_op jit(solution)/shard_map/ppermute | solution.py:19
  224.2 13.3 %copy-start.2 = (s32[64,16,256]{2,1,0:T(8,128)S(1)}, s32[64,16,256]{2,1,0:T(8,128)}, u32[]{:S(2)}) copy-start(s32[64,16,256]{2,1,0:T(8,128)} %param.10) | copy-start | bytes 3145732
  224.2 5.2 collective-permute-start
  229.5 5.3 collective-permute-start.2
  230.8 5.4 collective-permute-start.3
  283.0 18.4 %copy-start.1 = (f32[64,16,256]{2,1,0:T(8,128)}, f32[64,16,256]{2,1,0:T(8,128)S(1)}, u32[]{:S(2)}) copy-start(f32[64,16,256]{2,1,0:T(8,128)S(1)} %multiply_subtract_fusion) | copy-start | bytes 3145732
  283.0 7.0 %collective-permute-start.5 = (f32[1,16,256]{2,1,0:T(8,128)S(1)}, f32[1,16,256]{2,1,0:T(8,128)S(1)}, u32[]{:S(2)}, u32[]{:S(2)}) collective-permute-start(f32[1,16,256]{2,1,0:T(8,128)S(1)} %get-tuple-element.22), channel_id=1, source_target_pairs={{0,4},{4,8},{8,12},{12,16},{16,20},{20,24},{24,28},{1,5},{5,9},{9,... | collective-permute-start | bytes 49160 | tf_op jit(solution)/shard_map/ppermute | solution.py:19
  288.1 5.1 collective-permute-start.4
  293.3 8.2 %copy-start.3 = (s32[64,16,256]{2,1,0:T(8,128)S(1)}, s32[64,16,256]{2,1,0:T(8,128)}, u32[]{:S(2)}) copy-start(s32[64,16,256]{2,1,0:T(8,128)} %param.10) | copy-start | bytes 3145732
  293.3 5.5 collective-permute-start.6
  294.7 5.4 collective-permute-start.7
  349.6 1.0 copy-start.4
Sparse Core Ops, SparseCore 0:
  13.5 36.4 reduce-scatter.1
  52.4 32.8 all-reduce.6
  487.5 33.9 all-reduce.8
where the time goes:
time: 550 us; the launch traced here: 549 us
  other arithmetic  144 us (26%)
  local copies, waits for them, and re-layouts  141 us (26%)
  waiting for transfers between devices  113 us (21%)
  blocking collectives  93.9 us (17%)
  starting transfers between devices  25.6 us (5%)
  between operations  19.8 us (4%)
  matrix products  11.1 us (2%)
    gather x2, local copies, waits for them, and re-layouts, per_device(): jnp.take(potential.reshape(-1), flat_cell)  136 us
    scatter-add x1, other arithmetic, per_device(): jax.ops.segment_sum(jnp.where(inside, slab_occupancy, 0.0).reshape(-1), f...  129 us
    psum x2, blocking collectives, paired_sums(): lax.psum((jnp.sum(residual * residual), jnp.sum(residual * image)), ('ene...  80.7 us
    reduce_scatter x1, waiting for transfers between devices, per_device(): lax.psum_scatter(occupancy, 'energy', scatter_dimension=0, tiled=True)  35.4 us
    psum x1, waiting for transfers between devices, per_device(): slab_occupancy = lax.psum(partial_rows, 'kpt')  35.1 us
    psum x1, waiting for transfers between devices, per_device(): orbital_potential = lax.psum(local_values, 'kpt')  34.1 us
    ppermute x4, starting transfers between devices, with_halo(): lax.ppermute(lax.slice_in_dim(block, block.shape[dim] - width, None, axis...  18.8 us
    all_gather x1, blocking collectives, per_device(): lax.all_gather(orbital_potential, 'energy', axis=0, tiled=True)  13.3 us
  transfers between devices with their start and end apart: 11, of which 7 were waited for; matrix products, arithmetic and copies ran while one was open for 0% of the time, Pallas kernels for 0%

commit v1 on v0

v1 whole, which is shorter than its diff:
```python
import functools

import jax
import jax.numpy as jnp
from jax import lax
from jax.experimental import pallas as pl
from jax.experimental.pallas import tpu as pltpu
from jax.sharding import PartitionSpec as P

PENALTY = 4.0
MESH = pl.DeviceIdType.MESH
F32 = jnp.float32
BF16 = jnp.bfloat16
VMEM = pl.BlockSpec(memory_space=pltpu.VMEM)
SMEM = pl.BlockSpec(memory_space=pltpu.SMEM)
DMA = pltpu.SemaphoreType.DMA


def place():
    return lax.axis_index("energy"), lax.axis_index("kpt")


def enter(ne, nk):
    e, k = place()
    barrier = pltpu.get_barrier_semaphore()
    for step in range(1, ne):
        pl.semaphore_signal(
            barrier, inc=1, device_id=(lax.rem(e + step, ne), k), device_id_type=MESH
        )
    for step in range(1, nk):
        pl.semaphore_signal(
            barrier, inc=1, device_id=(e, lax.rem(k + step, nk)), device_id_type=MESH
        )
    pl.semaphore_wait(barrier, ne + nk - 2)


def send(src, dst, send_sem, recv_sem, target):
    copy = pltpu.make_async_remote_copy(
        src_ref=src,
        dst_ref=dst,
        send_sem=send_sem,
        recv_sem=recv_sem,
        device_id=target,
        device_id_type=MESH,
    )
    copy.start()
    return copy


def reduce_kernel(ne, nk, density, weights, out, mine, land, part, kland, es, er, ks, kr):
    e, k = place()
    points = density.shape[0]

    def slab_sum(t):
        total = weights[0, 0] * density[0, t].astype(F32)
        for q in range(1, points):
            total = total + weights[q, 0] * density[q, t].astype(F32)
        return total

    enter(ne, nk)
    copies = []
    for step in range(1, ne):
        t = lax.rem(e + step, ne)
        mine[step] = slab_sum(t)
        copies.append(send(mine.at[step], land.at[step], es.at[step], er.at[step], (t, k)))
    total = slab_sum(e)
    for step in range(1, ne):
        copies[step - 1].wait_recv()
        total = total + land[step]
    part[...] = total
    hops = []
    for step in range(1, nk):
        t = lax.rem(k + step, nk)
        hops.append(send(part, kland.at[step], ks.at[step], kr.at[step], (e, t)))
    for step in range(1, nk):
        hops[step - 1].wait_recv()
        total = total + kland[step]
    out[...] = total
    for copy in copies + hops:
        copy.wait_send()


def halves(values):
    high = values.astype(BF16)
    return high, (values - high.astype(F32)).astype(BF16)


def one_hot(count, index):
    iota = lax.broadcasted_iota(jnp.int32, (count, index.shape[1]), 0)
    return iota == index


def deposit_kernel(slab, sub, row_of, depth_of, occupancy, base, out):
    wy, nz = out.shape[1:]
    rows = sub * wy

    def layer(l, carry):
        hit = one_hot(rows, row_of[pl.ds(l, 1), :])
        value = occupancy[pl.ds(l, 1), :]
        high = value.astype(BF16).astype(F32)
        left = jnp.concatenate(
            [jnp.where(hit, high, 0.0).astype(BF16), jnp.where(hit, value - high, 0.0).astype(BF16)],
            axis=0,
        )
        right = jnp.where(one_hot(nz, depth_of[pl.ds(l, 1), :]), 1.0, 0.0).astype(BF16)
        both = lax.dot_general(left, right, (((1,), (1,)), ((), ())), preferred_element_type=F32)
        charge = (both[:rows] + both[rows:]).reshape(sub, wy, nz)
        out[pl.ds(l * sub, sub)] = base[pl.ds(l * sub, sub)] - charge
        return carry

    lax.fori_loop(0, slab, layer, 0)


def krylov_kernel(
    ne, nk, chunk, right_side, gate, image, stats, field, edge, halo, sums, eland, ksum, kland,
    xs, xr, ys, yr, es, er, ks, kr
):
    e, k = place()
    planes, wy, nz = right_side.shape
    enter(ne, nk)
    for v in range(2):
        @pl.when(e == 0)
        def _():
            field[v, 0] = jnp.zeros((wy, nz), F32)

        @pl.when(e == ne - 1)
        def _():
            field[v, planes + 1] = jnp.zeros((wy, nz), F32)

        @pl.when(k == 0)
        def _():
            halo[v, 0] = jnp.zeros((planes, nz), F32)

        @pl.when(k == nk - 1)
        def _():
            halo[v, 1] = jnp.zeros((planes, nz), F32)

    def fill(i, carry):
        b = i * chunk
        block = right_side[pl.ds(b, chunk)]
        field[0, pl.ds(b + 1, chunk)] = block
        edge[0, 0, pl.ds(b, chunk), :] = block[:, 0, :]
        edge[0, 1, pl.ds(b, chunk), :] = block[:, wy - 1, :]
        return carry

    lax.fori_loop(0, planes // chunk, fill, 0)

    def copies(v):
        def make(src, dst, ss, rs, target):
            return pltpu.make_async_remote_copy(
                src_ref=src, dst_ref=dst, send_sem=ss, recv_sem=rs,
                device_id=target, device_id_type=MESH,
            )

        up = make(field.at[v, planes], field.at[v, 0], xs.at[v, 0], xr.at[v, 0], (lax.rem(e + 1, ne), k))
        down = make(field.at[v, 1], field.at[v, planes + 1], xs.at[v, 1], xr.at[v, 1], (lax.rem(e + ne - 1, ne), k))
        right = make(edge.at[v, 1], halo.at[v, 0], ys.at[v, 0], yr.at[v, 0], (e, lax.rem(k + 1, nk)))
        left = make(edge.at[v, 0], halo.at[v, 1], ys.at[v, 1], yr.at[v, 1], (e, lax.rem(k + nk - 1, nk)))
        return ((up, e < ne - 1, e > 0), (down, e > 0, e < ne - 1), (right, k < nk - 1, k > 0), (left, k > 0, k < nk - 1))

    def start(v):
        for copy, sends, _ in copies(v):
            pl.when(sends)(copy.start)

    def arrive(v):
        for copy, _, receives in copies(v):
            pl.when(receives)(copy.wait_recv)

    row = lax.broadcasted_iota(jnp.int32, (chunk, wy, nz), 1)
    lane = lax.broadcasted_iota(jnp.int32, (chunk, wy, nz), 2)

    def applied(v, b):
        here = field[v, pl.ds(b + 1, chunk)]
        near = field[v, pl.ds(b, chunk)] + field[v, pl.ds(b + 2, chunk)]
        low = halo[v, 0, pl.ds(b, chunk), :].reshape(chunk, 1, nz)
        high = halo[v, 1, pl.ds(b, chunk), :].reshape(chunk, 1, nz)
        near = near + jnp.where(row == 0, low, pltpu.roll(here, 1, 1))
        near = near + jnp.where(row == wy - 1, high, pltpu.roll(here, wy - 1, 1))
        near = near + jnp.where(lane == 0, 0.0, pltpu.roll(here, 1, 2))
        near = near + jnp.where(lane == nz - 1, 0.0, pltpu.roll(here, nz - 1, 2))
        diagonal = 6.0 + PENALTY * gate[pl.ds(b, chunk)].astype(F32)
        return here, diagonal * here - near

    start(0)
    arrive(0)
    zero = jnp.zeros((wy, nz), F32)

    def first(i, carry):
        rr, rw, ww = carry
        b = i * chunk
        here, w = applied(0, b)
        field[1, pl.ds(b + 1, chunk)] = w
        image[pl.ds(b, chunk)] = w
        edge[1, 0, pl.ds(b, chunk), :] = w[:, 0, :]
        edge[1, 1, pl.ds(b, chunk), :] = w[:, wy - 1, :]
        return rr + jnp.sum(here * here, axis=0), rw + jnp.sum(here * w, axis=0), ww + jnp.sum(w * w, axis=0)

    rr, rw, ww = lax.fori_loop(0, planes // chunk, first, (zero, zero, zero))
    start(1)
    arrive(1)

    def second(i, wv):
        here, image_two = applied(1, i * chunk)
        return wv + jnp.sum(here * image_two, axis=0)

    wv = lax.fori_loop(0, planes // chunk, second, zero)
    sums[...] = jnp.zeros(sums.shape, F32)
    for i, acc in enumerate((rr, rw, ww, wv)):
        line = jnp.sum(acc, axis=0, keepdims=True)
        width = sums.shape[1]
        folded = line[:, :width]
        for at in range(width, nz, width):
            folded = folded + line[:, at : at + width]
        sums[i : i + 1, :] = folded
    outs = []
    for step in range(1, ne):
        outs.append(send(sums, eland.at[step], es.at[step], er.at[step], (lax.rem(e + step, ne), k)))
    total = sums[...]
    for step in range(1, ne):
        outs[step - 1].wait_recv()
        total = total + eland[step]
    ksum[...] = total
    for step in range(1, nk):
        outs.append(send(ksum, kland.at[step], ks.at[step], kr.at[step], (e, lax.rem(k + step, nk))))
    for step in range(1, nk):
        outs[ne - 2 + step].wait_recv()
        total = total + kland[step]
    stats[...] = total
    for copy in outs:
        copy.wait_send()
    for v in range(2):
        for copy, sends, _ in copies(v):
            pl.when(sends)(copy.wait_send)


def gather_kernel(slab, sub, nk, row_of, depth_of, right_side, image, stats, potential, local):
    wy, nz = right_side.shape[1:]
    rows = sub * wy
    sums = jnp.sum(stats[...], axis=1, keepdims=True)
    rr, rw, ww, wv = (sums[i : i + 1, :] for i in range(4))
    alpha = rr / rw
    norm_next = rr - 2.0 * alpha * rw + alpha * alpha * ww
    product = rw - 2.0 * alpha * ww + alpha * alpha * wv
    ratio = norm_next / rr
    alpha_two = norm_next / (product - ratio * norm_next / alpha)
    by_right = (alpha + alpha_two * (1.0 + ratio)).reshape(1, 1, 1)
    by_image = (alpha_two * alpha).reshape(1, 1, 1)
    cols = local.shape[2]

    def layer(l, carry):
        at = pl.ds(l * sub, sub)
        value = by_right * right_side[at] - by_image * image[at]
        potential[at] = value
        high, low = halves(value.reshape(rows, nz))
        left = jnp.concatenate([high, low], axis=0)
        right = jnp.where(one_hot(nz, depth_of[pl.ds(l, 1), :]), 1.0, 0.0).astype(BF16)
        both = jnp.dot(left, right, preferred_element_type=F32)
        hit = one_hot(rows, row_of[pl.ds(l, 1), :])
        picked = jnp.sum(jnp.where(hit, both[:rows] + both[rows:], 0.0), axis=0, keepdims=True)
        for j in range(nk):
            local[j, pl.ds(l, 1), :] = picked[:, j * cols : (j + 1) * cols]
        return carry

    lax.fori_loop(0, slab, layer, 0)


def shift_kernel(ne, nk, factor, local, density, out, kland, full, ks, kr, es, er, fs, fr):
    e, k = place()
    points = density.shape[0]
    cols = local.shape[2]
    enter(ne, nk)
    waits = []
    for step in range(1, nk):
        t = lax.rem(k + step, nk)
        waits.append(send(local.at[t], kland.at[step], ks.at[step], kr.at[step], (e, t)))
    piece = local[k]
    for step in range(1, nk):
        waits[step - 1].wait_recv()
        piece = piece + kland[step]
    full[k, e] = piece
    pieces = []
    for step in range(1, ne):
        pieces.append(
            send(full.at[k, e], full.at[k, e], es.at[step], er.at[step], (lax.rem(e + step, ne), k))
        )
    forwards = []
    for step in range(ne):
        owner = lax.rem(e + ne - step, ne)
        if step > 0:
            incoming = pltpu.make_async_remote_copy(
                src_ref=full.at[k, owner], dst_ref=full.at[k, owner],
                send_sem=es.at[step], recv_sem=er.at[step],
                device_id=(lax.rem(e + step, ne), k), device_id_type=MESH,
            )
            incoming.wait_recv()
        for hop in range(1, nk):
            forwards.append(
                send(full.at[k, owner], full.at[k, owner], fs.at[hop, step], fr.at[hop, step], (e, lax.rem(k + hop, nk)))
            )
    for step in range(ne):
        owner = lax.rem(e + ne - step, ne)
        for hop in range(1, nk):
            source = lax.rem(k + nk - hop, nk)
            pltpu.make_async_remote_copy(
                src_ref=full.at[source, owner], dst_ref=full.at[source, owner],
                send_sem=fs.at[hop, step], recv_sem=fr.at[hop, step],
                device_id=(e, lax.rem(k + hop, nk)), device_id_type=MESH,
            ).wait_recv()
    lane = lax.broadcasted_iota(jnp.int32, out.shape, 1)
    result = jnp.zeros(out.shape, F32)

    def one(t, result):
        for q in range(points):
            acc = jnp.zeros((out.shape[0], 1), F32)
            for j in range(nk):
                block = density[q, t, :, j * cols : (j + 1) * cols].astype(F32)
                acc = acc + jnp.sum(block * full[j, t], axis=1, keepdims=True)
            result = jnp.where(lane == q * ne + t, acc, result)
        return result

    out[...] = lax.fori_loop(0, ne, one, result) * factor
    for copy in waits + pieces + forwards:
        copy.wait_send()


def call(kernel, shapes, specs, scratch, args, number=None):
    params = {"vmem_limit_bytes": 48 * 1024 * 1024}
    if number is not None:
        params.update(collective_id=number, has_side_effects=True)
    return pl.pallas_call(
        kernel,
        out_shape=shapes,
        in_specs=specs,
        out_specs=jax.tree.map(lambda _: VMEM, shapes),
        scratch_shapes=scratch,
        compiler_params=pltpu.CompilerParams(**params),
    )(*args)


def per_device(density, quad_weights, orbital_cells, fixed_charge, gate_mask, gate_voltage):
    ne, nk = lax.axis_size("energy"), lax.axis_size("kpt")
    planes, wy, nz = fixed_charge.shape
    layers, orbitals = orbital_cells.shape
    points = density.shape[0]
    slab = layers // ne
    sub = planes // slab
    cols = orbitals // nk
    e, k = place()
    shape = jax.ShapeDtypeStruct
    blocks = density.reshape(points, ne, slab, orbitals)

    cells = lax.dynamic_slice_in_dim(orbital_cells, e * slab, slab, 0)
    section = wy * nk * nz
    within = cells % section
    column = within // nz - k * wy
    row_of = jnp.where((column >= 0) & (column < wy), (cells // section) * wy + column, -1)
    depth_of = within % nz
    gated = gate_mask.astype(F32)
    base = fixed_charge + PENALTY * gated * gate_voltage[:, None, None]

    occupancy = call(
        functools.partial(reduce_kernel, ne, nk),
        shape((slab, orbitals), F32),
        [VMEM, SMEM],
        [
            pltpu.VMEM((ne, slab, orbitals), F32),
            pltpu.VMEM((ne, slab, orbitals), F32),
            pltpu.VMEM((slab, orbitals), F32),
            pltpu.VMEM((nk, slab, orbitals), F32),
            DMA((ne,)), DMA((ne,)), DMA((nk,)), DMA((nk,)),
        ],
        (blocks, quad_weights),
        1,
    )
    right_side = call(
        functools.partial(deposit_kernel, slab, sub),
        shape((planes, wy, nz), F32),
        [VMEM] * 4,
        [],
        (row_of, depth_of, occupancy, base),
    )
    image, stats = call(
        functools.partial(krylov_kernel, ne, nk, 8),
        (shape((planes, wy, nz), F32), shape((8, 128), F32)),
        [VMEM] * 2,
        [
            pltpu.VMEM((2, planes + 2, wy, nz), F32),
            pltpu.VMEM((2, 2, planes, nz), F32),
            pltpu.VMEM((2, 2, planes, nz), F32),
            pltpu.VMEM((8, 128), F32),
            pltpu.VMEM((ne, 8, 128), F32),
            pltpu.VMEM((8, 128), F32),
            pltpu.VMEM((nk, 8, 128), F32),
            DMA((2, 2)), DMA((2, 2)), DMA((2, 2)), DMA((2, 2)),
            DMA((ne,)), DMA((ne,)), DMA((nk,)), DMA((nk,)),
        ],
        (right_side, gate_mask),
        2,
    )
    potential, local = call(
        functools.partial(gather_kernel, slab, sub, nk),
        (shape((planes, wy, nz), F32), shape((nk, slab, cols), F32)),
        [VMEM] * 5,
        [],
        (row_of, depth_of, right_side, image, stats),
    )
    shifts = call(
        functools.partial(shift_kernel, ne, nk, orbitals ** -0.5),
        shape((slab, 128), F32),
        [VMEM] * 2,
        [
            pltpu.VMEM((nk, slab, cols), F32),
            pltpu.VMEM((nk, ne, slab, cols), F32),
            DMA((nk,)), DMA((nk,)), DMA((ne,)), DMA((ne,)), DMA((nk, ne)), DMA((nk, ne)),
        ],
        (local, blocks),
        3,
    )
    band_shift = shifts[:, : points * ne].reshape(slab, points, ne)
    band_shift = band_shift.transpose(1, 2, 0).reshape(points, 1, layers)
    return potential, band_shift


def solution(mesh):
    in_specs = (
        P("energy", "kpt", None, None),
        P("energy", "kpt"),
        P(),
        P("energy", "kpt", None),
        P("energy", "kpt", None),
        P("energy"),
    )
    out_specs = (P("energy", "kpt", None), P("energy", "kpt", None))
    return jax.shard_map(
        per_device, mesh=mesh, in_specs=in_specs, out_specs=out_specs, check_vma=False
    )
```

time: 550 us -> 90 us (0.16)
  other arithmetic: 144 us -> 2.9 us
  local copies, waits for them, and re-layouts: 141 us -> 2.98 us
  waiting for transfers between devices: 113 us -> 0 us
  blocking collectives: 93.9 us -> 0 us
  Pallas kernels: 0 us -> 81.9 us
  starting transfers between devices: 25.6 us -> 0 us
  between operations: 19.8 us -> 0.71 us
  matrix products: 11.1 us -> 0 us
    gather x2 -> x0, local copies, waits for them, and re-layouts: 136 us -> none  [per_device(): jnp.take(potential.reshape(-1), flat_cell)]
    scatter-add x1 -> x0, other arithmetic: 129 us -> none  [per_device(): jax.ops.segment_sum(jnp.where(inside, slab_occupancy, 0.0).reshape(-1), f...]
    pallas_call x0 -> x5, Pallas kernels: none -> 81.9 us  [call(): pl.pallas_call(kernel, out_shape=shapes, in_specs=specs, out_specs=jax.tr...]
    psum x2 -> x0, blocking collectives: 80.7 us -> none  [paired_sums(): lax.psum((jnp.sum(residual * residual), jnp.sum(residual * image)), ('ene...]
    psum x2 -> x0, waiting for transfers between devices: 69.2 us -> none  [the longest x1 35.1 us: per_device(): slab_occupancy = lax.psum(partial_rows, 'kpt')]
    reduce_scatter x1 -> x0, waiting for transfers between devices: 35.4 us -> none  [per_device(): lax.psum_scatter(occupancy, 'energy', scatter_dimension=0, tiled=True)]
    ppermute x8 -> x0, starting transfers between devices: 25.5 us -> none  [the longest x4 18.8 us: with_halo(): lax.ppermute(lax.slice_in_dim(block, block.shape[dim] - width, None, axis...]
    all_gather x1 -> x0, blocking collectives: 13.3 us -> none  [per_device(): lax.all_gather(orbital_potential, 'energy', axis=0, tiled=True)]
  transfers between devices with their start and end apart: 11 -> 0, of which waited for: 7 -> 0; matrix products, arithmetic and copies ran while one was open for 0% -> 0% of each run, Pallas kernels for 0% -> 0%
where the time goes in v1:
time: 90 us; the launch traced here: 88.5 us
  Pallas kernels  81.9 us (91%)
  local copies, waits for them, and re-layouts  2.98 us (3%)
  other arithmetic  2.9 us (3%)
    pallas_call x5, Pallas kernels, call(): pl.pallas_call(kernel, out_shape=shapes, in_specs=specs, out_specs=jax.tr...  81.9 us
    unnamed x9, local copies, waits for them, and re-layouts  2.16 us

profile of v1, /device:TPU:1, one launch (start us, length us, event | category | flops | bytes accessed | tf_op | source)
XLA Modules:
  0.0 88.5 jit_solution(15706113325286550562)
XLA Ops:
  0.6 0.7 broadcast_multiply_fusion
  1.3 0.7 copy.8.weights
  2.0 0.0 copy-start
  2.0 1.4 %copy-done = bf16[4,1,64,3072]{3,2,1,0:T(8,128)(2,1)S(1)} copy-done((bf16[4,1,64,3072]{3,2,1,0:T(8,128)(2,1)S(1)}, bf16[4,1,64,3072]{3,2,1,0:T(8,128)(2,1)}, u32[]{:S(2)}) %copy-start) | copy-done | bytes 1572888
  3.4 0.0 copy-start.2
  3.4 0.0 copy-start.3
  3.4 23.9 %shard_map.77.occupancy = f32[8,3072]{1,0:T(8,128)S(1)} custom-call(bf16[4,8,8,3072]{3,2,1,0:T(8,128)(2,1)S(1)} %bitcast.3, f32[4,1]{1,0:T(4,128)S(1)} %copy.8.weights), custom_call_target="tpu_custom_call" | custom-call | tf_op jit(solution)/shard_map/pallas_call | solution.py:330
  27.3 1.0 %add_select_fusion = (s32[8,3072]{1,0:T(8,128)S(1)}, pred[8,3072]{1,0:T(8,128)(4,1)S(1)}) fusion(s32[64,3072]{1,0:T(8,128)} %param.8, s32[]{:T(128)S(6)} %select_n.26), kind=kLoop, calls=%fused_computation.1 | loop fusion | flops 540672 | bytes 221188 | tf_op jit(solution)/shard_map/jit(remainder)/select_n | solution.py:357
  28.3 1.1 %fusion.3.row_of = s32[8,3072]{1,0:T(8,128)S(1)} fusion(pred[8,3072]{1,0:T(8,128)(4,1)S(1)} %get-tuple-element.11, s32[64,3072]{1,0:T(8,128)} %param.8, s32[]{:T(128)S(6)} %select_n.26, s32[]{:T(128)S(6)} %mul.24), kind=kLoop, calls=%fused_computation.14 | loop fusion | flops 983040 | bytes 221192 | tf_op jit(solution)/shard_map/jit(_where)/select_n | solution.py:356
  29.4 0.0 copy-done.2
  29.4 0.0 copy-done.3
  29.4 0.2 multiply_add_fusion.base
  29.6 5.8 %shard_map.78.right_side = f32[64,16,256]{2,1,0:T(8,128)S(1)} custom-call(s32[8,3072]{1,0:T(8,128)S(1)} %fusion.3.row_of, s32[8,3072]{1,0:T(8,128)S(1)} %get-tuple-element.10.depth_of, f32[8,3072]{1,0:T(8,128)S(1)} %shard_map.77.occupancy, f32[64,16,256]{2,1,0:T(8,128)S(1)} %multiply_add_fusion.base), custom_call_target="tpu_custom_call" | custom-call | tf_op jit(solution)/shard_map/pallas_call | solution.py:330
  35.4 18.8 %shard_map.79 = (f32[64,16,256]{2,1,0:T(8,128)S(1)}, f32[8,128]{1,0:T(8,128)S(1)}) custom-call(f32[64,16,256]{2,1,0:T(8,128)S(1)} %shard_map.78.right_side, s32[64,16,256]{2,1,0:T(8,128)S(1)} %copy-done.2), custom_call_target="tpu_custom_call" | custom-call | tf_op jit(solution)/shard_map/pallas_call | solution.py:330
  54.2 0.0 copy-start.1
  54.2 7.2 %shard_map.80 = (f32[64,16,256]{2,1,0:T(8,128)}, f32[4,8,768]{2,1,0:T(8,128)S(1)}) custom-call(s32[8,3072]{1,0:T(8,128)S(1)} %fusion.3.row_of, s32[8,3072]{1,0:T(8,128)S(1)} %get-tuple-element.10.depth_of, f32[64,16,256]{2,1,0:T(8,128)S(1)} %shard_map.78.right_side, f32[64,16,256]{2,1,0:T(8,128)S(1)} %get-tuple-element.6.image, ...), custom_call_target="tpu_custom_call" | custom-call | tf_op jit(solution)/shard_map/pallas_call | solution.py:330
  61.4 0.0 copy-done.1
  61.4 26.2 %shard_map.81 = f32[8,128]{1,0:T(8,128)S(1)} custom-call(f32[4,8,768]{2,1,0:T(8,128)S(1)} %get-tuple-element.9.local, bf16[4,8,8,3072]{3,2,1,0:T(8,128)(2,1)S(1)} %bitcast.4), custom_call_target="tpu_custom_call" | custom-call | tf_op jit(solution)/shard_map/pallas_call | solution.py:330
  87.6 0.1 reshape.15
  87.7 0.1 copy.9
  87.8 0.7 reshape.16
Async XLA Ops:
  2.0 1.4 %copy-start = (bf16[4,1,64,3072]{3,2,1,0:T(8,128)(2,1)S(1)}, bf16[4,1,64,3072]{3,2,1,0:T(8,128)(2,1)}, u32[]{:S(2)}) copy-start(bf16[4,1,64,3072]{3,2,1,0:T(8,128)(2,1)} %param.6) | copy-start | bytes 4718596
  3.4 25.9 %copy-start.2 = (s32[64,16,256]{2,1,0:T(8,128)S(1)}, s32[64,16,256]{2,1,0:T(8,128)}, u32[]{:S(2)}) copy-start(s32[64,16,256]{2,1,0:T(8,128)} %gate.1) | copy-start | bytes 3145732
  3.4 25.9 %copy-start.3 = (f32[64,16,256]{2,1,0:T(8,128)S(1)}, f32[64,16,256]{2,1,0:T(8,128)}, u32[]{:S(2)}) copy-start(f32[64,16,256]{2,1,0:T(8,128)} %param.9) | copy-start | bytes 3145732
  54.2 7.2 %copy-start.1 = (bf16[4,1,64,3072]{3,2,1,0:T(8,128)(2,1)S(1)}, bf16[4,1,64,3072]{3,2,1,0:T(8,128)(2,1)}, u32[]{:S(2)}) copy-start(bf16[4,1,64,3072]{3,2,1,0:T(8,128)(2,1)} %param.6) | copy-start | bytes 4718596

commit v2 on v1

--- a/solution.py
+++ b/solution.py
@@ -264,7 +264,7 @@
     lax.fori_loop(0, slab, layer, 0)
 
 
-def shift_kernel(ne, nk, factor, local, density, out, kland, full, ks, kr, es, er, fs, fr):
+def shift_kernel(ne, nk, factor, local, density, out, kland, full, ks, kr, es, er, fs, fr, gs, gr):
     e, k = place()
     points = density.shape[0]
     cols = local.shape[2]
@@ -278,34 +278,34 @@
         waits[step - 1].wait_recv()
         piece = piece + kland[step]
     full[k, e] = piece
-    pieces = []
-    for step in range(1, ne):
-        pieces.append(
-            send(full.at[k, e], full.at[k, e], es.at[step], er.at[step], (lax.rem(e + step, ne), k))
+    pieces = [None] * ne
+    evens, odds = range(0, ne, 2), range(1, ne, 2)
+    partner = e + 1 - 2 * lax.rem(e, 2)
+    for step in [*evens[1:], *odds]:
+        pieces[step] = send(
+            full.at[k, e], full.at[k, e], es.at[step], er.at[step], (lax.rem(e + step, ne), k)
         )
     forwards = []
-    for step in range(ne):
+    for step in evens:
         owner = lax.rem(e + ne - step, ne)
         if step > 0:
-            incoming = pltpu.make_async_remote_copy(
-                src_ref=full.at[k, owner], dst_ref=full.at[k, owner],
-                send_sem=es.at[step], recv_sem=er.at[step],
-                device_id=(lax.rem(e + step, ne), k), device_id_type=MESH,
-            )
-            incoming.wait_recv()
+            pieces[step].wait_recv()
         for hop in range(1, nk):
             forwards.append(
                 send(full.at[k, owner], full.at[k, owner], fs.at[hop, step], fr.at[hop, step], (e, lax.rem(k + hop, nk)))
             )
-    for step in range(ne):
+    for step in odds:
+        pieces[step].wait_recv()
+    at = 0
+    for step in evens:
         owner = lax.rem(e + ne - step, ne)
         for hop in range(1, nk):
-            source = lax.rem(k + nk - hop, nk)
-            pltpu.make_async_remote_copy(
-                src_ref=full.at[source, owner], dst_ref=full.at[source, owner],
-                send_sem=fs.at[hop, step], recv_sem=fr.at[hop, step],
-                device_id=(e, lax.rem(k + hop, nk)), device_id_type=MESH,
-            ).wait_recv()
+            forwards[at].wait_recv()
+            at += 1
+            here = full.at[lax.rem(k + nk - hop, nk), owner]
+            forwards.append(send(here, here, gs.at[hop, step], gr.at[hop, step], (partner, k)))
+    for copy in forwards[at:]:
+        copy.wait_recv()
     lane = lax.broadcasted_iota(jnp.int32, out.shape, 1)
     result = jnp.zeros(out.shape, F32)
 
@@ -319,7 +319,7 @@
         return result
 
     out[...] = lax.fori_loop(0, ne, one, result) * factor
-    for copy in waits + pieces + forwards:
+    for copy in waits + pieces[1:] + forwards:
         copy.wait_send()
 
 
@@ -411,7 +411,8 @@
         [
             pltpu.VMEM((nk, slab, cols), F32),
             pltpu.VMEM((nk, ne, slab, cols), F32),
-            DMA((nk,)), DMA((nk,)), DMA((ne,)), DMA((ne,)), DMA((nk, ne)), DMA((nk, ne)),
+            DMA((nk,)), DMA((nk,)), DMA((ne,)), DMA((ne,)),
+            DMA((nk, ne)), DMA((nk, ne)), DMA((nk, ne)), DMA((nk, ne)),
         ],
         (local, blocks),
         3,

time: 90 us -> 83.1 us (0.923); the launches traced: 88.5 us -> 82.9 us
  Pallas kernels: 81.9 us -> 76.3 us
    pallas_call x5, Pallas kernels: 81.9 us -> 76.3 us  [call(): pl.pallas_call(kernel, out_shape=shapes, in_specs=specs, out_specs=jax.tr...]
where the time goes in v2:
time: 83.1 us; the launch traced here: 82.9 us
  Pallas kernels  76.3 us (92%)
  local copies, waits for them, and re-layouts  2.98 us (4%)
  other arithmetic  2.9 us (3%)
    pallas_call x5, Pallas kernels, call(): pl.pallas_call(kernel, out_shape=shapes, in_specs=specs, out_specs=jax.tr...  76.3 us
    unnamed x9, local copies, waits for them, and re-layouts  2.16 us

profile of v2, /device:TPU:1, one launch (start us, length us, event | category | flops | bytes accessed | tf_op | source)
XLA Modules:
  0.0 82.9 jit_solution(7438531126169619759)
XLA Ops:
  0.6 0.7 broadcast_multiply_fusion
  1.3 0.7 copy.8.weights
  2.0 0.0 copy-start
  2.0 1.4 %copy-done = bf16[4,1,64,3072]{3,2,1,0:T(8,128)(2,1)S(1)} copy-done((bf16[4,1,64,3072]{3,2,1,0:T(8,128)(2,1)S(1)}, bf16[4,1,64,3072]{3,2,1,0:T(8,128)(2,1)}, u32[]{:S(2)}) %copy-start) | copy-done | bytes 1572888
  3.4 0.0 copy-start.2
  3.4 0.0 copy-start.3
  3.4 23.9 %shard_map.77.occupancy = f32[8,3072]{1,0:T(8,128)S(1)} custom-call(bf16[4,8,8,3072]{3,2,1,0:T(8,128)(2,1)S(1)} %bitcast.3, f32[4,1]{1,0:T(4,128)S(1)} %copy.8.weights), custom_call_target="tpu_custom_call" | custom-call | tf_op jit(solution)/shard_map/pallas_call | solution.py:330
  27.3 1.0 %add_select_fusion = (s32[8,3072]{1,0:T(8,128)S(1)}, pred[8,3072]{1,0:T(8,128)(4,1)S(1)}) fusion(s32[64,3072]{1,0:T(8,128)} %param.8, s32[]{:T(128)S(6)} %select_n.26), kind=kLoop, calls=%fused_computation.1 | loop fusion | flops 540672 | bytes 221188 | tf_op jit(solution)/shard_map/jit(remainder)/select_n | solution.py:357
  28.3 1.1 %fusion.3.row_of = s32[8,3072]{1,0:T(8,128)S(1)} fusion(pred[8,3072]{1,0:T(8,128)(4,1)S(1)} %get-tuple-element.11, s32[64,3072]{1,0:T(8,128)} %param.8, s32[]{:T(128)S(6)} %select_n.26, s32[]{:T(128)S(6)} %mul.24), kind=kLoop, calls=%fused_computation.14 | loop fusion | flops 983040 | bytes 221192 | tf_op jit(solution)/shard_map/jit(_where)/select_n | solution.py:356
  29.4 0.0 copy-done.2
  29.4 0.0 copy-done.3
  29.4 0.2 multiply_add_fusion.base
  29.6 5.8 %shard_map.78.right_side = f32[64,16,256]{2,1,0:T(8,128)S(1)} custom-call(s32[8,3072]{1,0:T(8,128)S(1)} %fusion.3.row_of, s32[8,3072]{1,0:T(8,128)S(1)} %get-tuple-element.10.depth_of, f32[8,3072]{1,0:T(8,128)S(1)} %shard_map.77.occupancy, f32[64,16,256]{2,1,0:T(8,128)S(1)} %multiply_add_fusion.base), custom_call_target="tpu_custom_call" | custom-call | tf_op jit(solution)/shard_map/pallas_call | solution.py:330
  35.4 18.8 %shard_map.79 = (f32[64,16,256]{2,1,0:T(8,128)S(1)}, f32[8,128]{1,0:T(8,128)S(1)}) custom-call(f32[64,16,256]{2,1,0:T(8,128)S(1)} %shard_map.78.right_side, s32[64,16,256]{2,1,0:T(8,128)S(1)} %copy-done.2), custom_call_target="tpu_custom_call" | custom-call | tf_op jit(solution)/shard_map/pallas_call | solution.py:330
  54.2 0.0 copy-start.1
  54.2 7.2 %shard_map.80 = (f32[64,16,256]{2,1,0:T(8,128)}, f32[4,8,768]{2,1,0:T(8,128)S(1)}) custom-call(s32[8,3072]{1,0:T(8,128)S(1)} %fusion.3.row_of, s32[8,3072]{1,0:T(8,128)S(1)} %get-tuple-element.10.depth_of, f32[64,16,256]{2,1,0:T(8,128)S(1)} %shard_map.78.right_side, f32[64,16,256]{2,1,0:T(8,128)S(1)} %get-tuple-element.6.image, ...), custom_call_target="tpu_custom_call" | custom-call | tf_op jit(solution)/shard_map/pallas_call | solution.py:330
  61.4 0.0 copy-done.1
  61.4 20.6 %shard_map.81 = f32[8,128]{1,0:T(8,128)S(1)} custom-call(f32[4,8,768]{2,1,0:T(8,128)S(1)} %get-tuple-element.9.local, bf16[4,8,8,3072]{3,2,1,0:T(8,128)(2,1)S(1)} %bitcast.4), custom_call_target="tpu_custom_call" | custom-call | tf_op jit(solution)/shard_map/pallas_call | solution.py:330
  82.1 0.1 reshape.15
  82.2 0.1 copy.9
  82.2 0.7 reshape.16
Async XLA Ops:
  2.0 1.4 %copy-start = (bf16[4,1,64,3072]{3,2,1,0:T(8,128)(2,1)S(1)}, bf16[4,1,64,3072]{3,2,1,0:T(8,128)(2,1)}, u32[]{:S(2)}) copy-start(bf16[4,1,64,3072]{3,2,1,0:T(8,128)(2,1)} %param.6) | copy-start | bytes 4718596
  3.4 25.9 %copy-start.2 = (s32[64,16,256]{2,1,0:T(8,128)S(1)}, s32[64,16,256]{2,1,0:T(8,128)}, u32[]{:S(2)}) copy-start(s32[64,16,256]{2,1,0:T(8,128)} %gate.1) | copy-start | bytes 3145732
  3.4 25.9 %copy-start.3 = (f32[64,16,256]{2,1,0:T(8,128)S(1)}, f32[64,16,256]{2,1,0:T(8,128)}, u32[]{:S(2)}) copy-start(f32[64,16,256]{2,1,0:T(8,128)} %param.9) | copy-start | bytes 3145732
  54.2 7.2 %copy-start.1 = (bf16[4,1,64,3072]{3,2,1,0:T(8,128)(2,1)S(1)}, bf16[4,1,64,3072]{3,2,1,0:T(8,128)(2,1)}, u32[]{:S(2)}) copy-start(bf16[4,1,64,3072]{3,2,1,0:T(8,128)(2,1)} %param.6) | copy-start | bytes 4718596

commit v3 on v2

--- a/solution.py
+++ b/solution.py
@@ -58,14 +58,26 @@
         return total
 
     enter(ne, nk)
+    partner = e + 1 - 2 * lax.rem(e, 2)
+    order = [*range(2, ne, 2), 0]
+    shares = []
+    for step in order:
+        mine[step + 1] = slab_sum(lax.rem(partner + step, ne))
+        shares.append(
+            send(mine.at[step + 1], land.at[step + 1], es.at[step + 1], er.at[step + 1], (partner, k))
+        )
     copies = []
-    for step in range(1, ne):
+    for share, step in zip(shares[:-1], order[:-1]):
         t = lax.rem(e + step, ne)
-        mine[step] = slab_sum(t)
+        value = slab_sum(t)
+        share.wait_recv()
+        mine[step] = value + land[step + 1]
         copies.append(send(mine.at[step], land.at[step], es.at[step], er.at[step], (t, k)))
     total = slab_sum(e)
-    for step in range(1, ne):
-        copies[step - 1].wait_recv()
+    shares[-1].wait_recv()
+    total = total + land[1]
+    for copy, step in zip(copies, order[:-1]):
+        copy.wait_recv()
         total = total + land[step]
     part[...] = total
     hops = []
@@ -76,7 +88,7 @@
         hops[step - 1].wait_recv()
         total = total + kland[step]
     out[...] = total
-    for copy in copies + hops:
+    for copy in shares + copies + hops:
         copy.wait_send()
 
 

time: 83.1 us -> 81 us (0.975)
  Pallas kernels: 76.3 us -> 74.2 us
    pallas_call x5, Pallas kernels: 76.3 us -> 74.2 us  [call(): pl.pallas_call(kernel, out_shape=shapes, in_specs=specs, out_specs=jax.tr...]
where the time goes in v3:
time: 81 us; the launch traced here: 80.8 us
  Pallas kernels  74.2 us (92%)
  local copies, waits for them, and re-layouts  2.98 us (4%)
  other arithmetic  2.9 us (4%)
    pallas_call x5, Pallas kernels, call(): pl.pallas_call(kernel, out_shape=shapes, in_specs=specs, out_specs=jax.tr...  74.2 us
    unnamed x9, local copies, waits for them, and re-layouts  2.16 us

profile of v3, /device:TPU:1, one launch (start us, length us, event | category | flops | bytes accessed | tf_op | source)
XLA Modules:
  0.0 80.8 jit_solution(15683274042566689024)
XLA Ops:
  0.6 0.7 broadcast_multiply_fusion
  1.3 0.7 copy.8.weights
  2.0 0.0 copy-start
  2.0 1.4 %copy-done = bf16[4,1,64,3072]{3,2,1,0:T(8,128)(2,1)S(1)} copy-done((bf16[4,1,64,3072]{3,2,1,0:T(8,128)(2,1)S(1)}, bf16[4,1,64,3072]{3,2,1,0:T(8,128)(2,1)}, u32[]{:S(2)}) %copy-start) | copy-done | bytes 1572888
  3.4 0.0 copy-start.2
  3.4 0.0 copy-start.3
  3.4 20.5 %shard_map.77.occupancy = f32[8,3072]{1,0:T(8,128)S(1)} custom-call(bf16[4,8,8,3072]{3,2,1,0:T(8,128)(2,1)S(1)} %bitcast.3, f32[4,1]{1,0:T(4,128)S(1)} %copy.8.weights), custom_call_target="tpu_custom_call" | custom-call | tf_op jit(solution)/shard_map/pallas_call | solution.py:342
  23.9 1.0 %add_select_fusion = (s32[8,3072]{1,0:T(8,128)S(1)}, pred[8,3072]{1,0:T(8,128)(4,1)S(1)}) fusion(s32[64,3072]{1,0:T(8,128)} %param.8, s32[]{:T(128)S(6)} %select_n.26), kind=kLoop, calls=%fused_computation.1 | loop fusion | flops 540672 | bytes 221188 | tf_op jit(solution)/shard_map/jit(remainder)/select_n | solution.py:369
  24.9 1.1 %fusion.3.row_of = s32[8,3072]{1,0:T(8,128)S(1)} fusion(pred[8,3072]{1,0:T(8,128)(4,1)S(1)} %get-tuple-element.11, s32[64,3072]{1,0:T(8,128)} %param.8, s32[]{:T(128)S(6)} %select_n.26, s32[]{:T(128)S(6)} %mul.24), kind=kLoop, calls=%fused_computation.14 | loop fusion | flops 983040 | bytes 221192 | tf_op jit(solution)/shard_map/jit(_where)/select_n | solution.py:368
  26.0 0.0 copy-done.2
  26.0 0.0 copy-done.3
  26.0 0.2 multiply_add_fusion.base
  26.2 5.8 %shard_map.78.right_side = f32[64,16,256]{2,1,0:T(8,128)S(1)} custom-call(s32[8,3072]{1,0:T(8,128)S(1)} %fusion.3.row_of, s32[8,3072]{1,0:T(8,128)S(1)} %get-tuple-element.10.depth_of, f32[8,3072]{1,0:T(8,128)S(1)} %shard_map.77.occupancy, f32[64,16,256]{2,1,0:T(8,128)S(1)} %multiply_add_fusion.base), custom_call_target="tpu_custom_call" | custom-call | tf_op jit(solution)/shard_map/pallas_call | solution.py:342
  32.0 20.1 %shard_map.79 = (f32[64,16,256]{2,1,0:T(8,128)S(1)}, f32[8,128]{1,0:T(8,128)S(1)}) custom-call(f32[64,16,256]{2,1,0:T(8,128)S(1)} %shard_map.78.right_side, s32[64,16,256]{2,1,0:T(8,128)S(1)} %copy-done.2), custom_call_target="tpu_custom_call" | custom-call | tf_op jit(solution)/shard_map/pallas_call | solution.py:342
  52.1 0.0 copy-start.1
  52.1 7.2 %shard_map.80 = (f32[64,16,256]{2,1,0:T(8,128)}, f32[4,8,768]{2,1,0:T(8,128)S(1)}) custom-call(s32[8,3072]{1,0:T(8,128)S(1)} %fusion.3.row_of, s32[8,3072]{1,0:T(8,128)S(1)} %get-tuple-element.10.depth_of, f32[64,16,256]{2,1,0:T(8,128)S(1)} %shard_map.78.right_side, f32[64,16,256]{2,1,0:T(8,128)S(1)} %get-tuple-element.6.image, ...), custom_call_target="tpu_custom_call" | custom-call | tf_op jit(solution)/shard_map/pallas_call | solution.py:342
  59.3 0.0 copy-done.1
  59.3 20.7 %shard_map.81 = f32[8,128]{1,0:T(8,128)S(1)} custom-call(f32[4,8,768]{2,1,0:T(8,128)S(1)} %get-tuple-element.9.local, bf16[4,8,8,3072]{3,2,1,0:T(8,128)(2,1)S(1)} %bitcast.4), custom_call_target="tpu_custom_call" | custom-call | tf_op jit(solution)/shard_map/pallas_call | solution.py:342
  80.0 0.1 reshape.15
  80.1 0.1 copy.9
  80.2 0.7 reshape.16
Async XLA Ops:
  2.0 1.4 %copy-start = (bf16[4,1,64,3072]{3,2,1,0:T(8,128)(2,1)S(1)}, bf16[4,1,64,3072]{3,2,1,0:T(8,128)(2,1)}, u32[]{:S(2)}) copy-start(bf16[4,1,64,3072]{3,2,1,0:T(8,128)(2,1)} %param.6) | copy-start | bytes 4718596
  3.4 22.5 %copy-start.2 = (s32[64,16,256]{2,1,0:T(8,128)S(1)}, s32[64,16,256]{2,1,0:T(8,128)}, u32[]{:S(2)}) copy-start(s32[64,16,256]{2,1,0:T(8,128)} %gate.1) | copy-start | bytes 3145732
  3.4 22.5 %copy-start.3 = (f32[64,16,256]{2,1,0:T(8,128)S(1)}, f32[64,16,256]{2,1,0:T(8,128)}, u32[]{:S(2)}) copy-start(f32[64,16,256]{2,1,0:T(8,128)} %param.9) | copy-start | bytes 3145732
  52.1 7.2 %copy-start.1 = (bf16[4,1,64,3072]{3,2,1,0:T(8,128)(2,1)S(1)}, bf16[4,1,64,3072]{3,2,1,0:T(8,128)(2,1)}, u32[]{:S(2)}) copy-start(bf16[4,1,64,3072]{3,2,1,0:T(8,128)(2,1)} %param.6) | copy-start | bytes 4718596

commit v4 on v3

--- a/solution.py
+++ b/solution.py
@@ -102,9 +102,14 @@
     return iota == index
 
 
-def deposit_kernel(slab, sub, row_of, depth_of, occupancy, base, out):
+def deposit_kernel(slab, sub, nk, cells, occupancy, base, out, row_of, depth_of):
     wy, nz = out.shape[1:]
     rows = sub * wy
+    line = lax.div(cells[...], nz)
+    depth_of[...] = cells[...] - line * nz
+    plane = lax.div(line, wy * nk)
+    column = line - plane * (wy * nk) - lax.axis_index("kpt") * wy
+    row_of[...] = jnp.where((column >= 0) & (column < wy), plane * wy + column, -1)
 
     def layer(l, carry):
         hit = one_hot(rows, row_of[pl.ds(l, 1), :])
@@ -357,16 +362,11 @@
     slab = layers // ne
     sub = planes // slab
     cols = orbitals // nk
-    e, k = place()
+    e = lax.axis_index("energy")
     shape = jax.ShapeDtypeStruct
     blocks = density.reshape(points, ne, slab, orbitals)
 
     cells = lax.dynamic_slice_in_dim(orbital_cells, e * slab, slab, 0)
-    section = wy * nk * nz
-    within = cells % section
-    column = within // nz - k * wy
-    row_of = jnp.where((column >= 0) & (column < wy), (cells // section) * wy + column, -1)
-    depth_of = within % nz
     gated = gate_mask.astype(F32)
     base = fixed_charge + PENALTY * gated * gate_voltage[:, None, None]
 
@@ -384,12 +384,12 @@
         (blocks, quad_weights),
         1,
     )
-    right_side = call(
-        functools.partial(deposit_kernel, slab, sub),
-        shape((planes, wy, nz), F32),
-        [VMEM] * 4,
+    right_side, row_of, depth_of = call(
+        functools.partial(deposit_kernel, slab, sub, nk),
+        (shape((planes, wy, nz), F32), *[shape((slab, orbitals), jnp.int32)] * 2),
+        [VMEM] * 3,
         [],
-        (row_of, depth_of, occupancy, base),
+        (cells, occupancy, base),
     )
     image, stats = call(
         functools.partial(krylov_kernel, ne, nk, 8),

time: 81 us -> 80.3 us (level)
    select_n x2 -> x0, other arithmetic: 2.06 us -> none  [the longest x1 1.07 us: per_device(): jnp.where((column >= 0) & (column < wy), cells // section * wy + column, -1)]
    add x1, other arithmetic: 0.18 us -> 1.4 us  [per_device(): base = fixed_charge + PENALTY * gated * gate_voltage[:, None, None]]
where the time goes in v4:
time: 80.3 us; the launch traced here: 80.1 us
  Pallas kernels  74.3 us (93%)
  local copies, waits for them, and re-layouts  3.01 us (4%)
  other arithmetic  2.13 us (3%)
    pallas_call x5, Pallas kernels, call(): pl.pallas_call(kernel, out_shape=shapes, in_specs=specs, out_specs=jax.tr...  74.3 us
    unnamed x9, local copies, waits for them, and re-layouts  2.17 us

profile of v4, /device:TPU:1, one launch (start us, length us, event | category | flops | bytes accessed | tf_op | source)
XLA Modules:
  0.0 80.1 jit_solution(5364270770704110982)
XLA Ops:
  0.6 0.0 copy-start
  0.7 0.7 broadcast_multiply_fusion
  1.4 0.7 copy.8.weights
  2.1 0.0 copy-start.1
  2.1 1.4 %copy-done.1 = bf16[4,1,64,3072]{3,2,1,0:T(8,128)(2,1)S(1)} copy-done((bf16[4,1,64,3072]{3,2,1,0:T(8,128)(2,1)S(1)}, bf16[4,1,64,3072]{3,2,1,0:T(8,128)(2,1)}, u32[]{:S(2)}) %copy-start.1) | copy-done | bytes 1572888
  3.5 0.0 copy-start.3
  3.5 20.5 %shard_map.77.occupancy = f32[8,3072]{1,0:T(8,128)S(1)} custom-call(bf16[4,8,8,3072]{3,2,1,0:T(8,128)(2,1)S(1)} %bitcast.3, f32[4,1]{1,0:T(4,128)S(1)} %copy.8.weights), custom_call_target="tpu_custom_call" | custom-call | tf_op jit(solution)/shard_map/pallas_call | solution.py:347
  24.0 0.0 copy-done
  24.0 0.0 copy-done.3
  24.1 1.4 %multiply_add_fusion.base = f32[64,16,256]{2,1,0:T(8,128)S(1)} fusion(f32[64,16,256]{2,1,0:T(8,128)} %param.9, s32[64,16,256]{2,1,0:T(8,128)S(1)} %copy-done.3, f32[64]{0:T(128)S(1)} %broadcast_multiply_fusion), kind=kLoop, calls=%fused_computation | loop fusion | flops 786432 | bytes 3145984 | tf_op jit(solution)/shard_map/add | solution.py:371
  25.5 5.9 %shard_map.78 = (f32[64,16,256]{2,1,0:T(8,128)S(1)}, s32[8,3072]{1,0:T(8,128)S(1)}, s32[8,3072]{1,0:T(8,128)S(1)}) custom-call(s32[8,3072]{1,0:T(8,128)S(1)} %constant_dynamic-slice_fusion.cells, f32[8,3072]{1,0:T(8,128)S(1)} %shard_map.77.occupancy, f32[64,16,256]{2,1,0:T(8,128)S(1)} %multiply_add_fusion.base), custom_call_target="tpu_custom_call" | custom-call | tf_op jit(solution)/shard_map/pallas_call | solution.py:347
  31.3 20.1 %shard_map.79 = (f32[64,16,256]{2,1,0:T(8,128)S(1)}, f32[8,128]{1,0:T(8,128)S(1)}) custom-call(f32[64,16,256]{2,1,0:T(8,128)S(1)} %get-tuple-element.11.right_side, s32[64,16,256]{2,1,0:T(8,128)S(1)} %copy-done.3), custom_call_target="tpu_custom_call" | custom-call | tf_op jit(solution)/shard_map/pallas_call | solution.py:347
  51.4 0.0 copy-start.2
  51.4 7.2 %shard_map.80 = (f32[64,16,256]{2,1,0:T(8,128)}, f32[4,8,768]{2,1,0:T(8,128)S(1)}) custom-call(s32[8,3072]{1,0:T(8,128)S(1)} %get-tuple-element.9.row_of, s32[8,3072]{1,0:T(8,128)S(1)} %get-tuple-element.10.depth_of, f32[64,16,256]{2,1,0:T(8,128)S(1)} %get-tuple-element.11.right_side, f32[64,16,256]{2,1,0:T(8,128)S(1)} %get-tuple-element.12.image, ...), custom_call_target="tpu_custom_call" | custom-call | tf_op jit(solution)/shard_map/pallas_call | solution.py:347
  58.6 0.0 copy-done.2
  58.6 20.7 %shard_map.81 = f32[8,128]{1,0:T(8,128)S(1)} custom-call(f32[4,8,768]{2,1,0:T(8,128)S(1)} %get-tuple-element.15.local, bf16[4,8,8,3072]{3,2,1,0:T(8,128)(2,1)S(1)} %bitcast.4), custom_call_target="tpu_custom_call" | custom-call | tf_op jit(solution)/shard_map/pallas_call | solution.py:347
  79.3 0.1 reshape.15
  79.4 0.1 copy.9
  79.5 0.7 reshape.16
  (1 shorter events, 0.0 us)
Async XLA Ops:
  0.6 23.4 %copy-start = (s32[64,3072]{1,0:T(8,128)S(1)}, s32[64,3072]{1,0:T(8,128)}, u32[]{:S(2)}) copy-start(s32[64,3072]{1,0:T(8,128)} %param.8) | copy-start | bytes 2359300
  2.1 1.4 %copy-start.1 = (bf16[4,1,64,3072]{3,2,1,0:T(8,128)(2,1)S(1)}, bf16[4,1,64,3072]{3,2,1,0:T(8,128)(2,1)}, u32[]{:S(2)}) copy-start(bf16[4,1,64,3072]{3,2,1,0:T(8,128)(2,1)} %param.6) | copy-start | bytes 4718596
  3.5 20.5 %copy-start.3 = (s32[64,16,256]{2,1,0:T(8,128)S(1)}, s32[64,16,256]{2,1,0:T(8,128)}, u32[]{:S(2)}) copy-start(s32[64,16,256]{2,1,0:T(8,128)} %gate.1) | copy-start | bytes 3145732
  51.4 7.2 %copy-start.2 = (bf16[4,1,64,3072]{3,2,1,0:T(8,128)(2,1)S(1)}, bf16[4,1,64,3072]{3,2,1,0:T(8,128)(2,1)}, u32[]{:S(2)}) copy-start(bf16[4,1,64,3072]{3,2,1,0:T(8,128)(2,1)} %param.6) | copy-start | bytes 4718596
